TPU v7x, 32 devices: a whole 2x2x4 slice. The times are simulated.
32 devices in a mesh: dp: 16 (over z, x, core), vol: 2 (over y).
Axes of the slice: x: 2, y: 2, z: 4, core: 2. Of those that a mesh axis runs over, the one named last changes fastest.
Arguments:
- images: float32 [32, 128, 128], P(('dp', 'vol')), may hold values from -6 to 6
- contrast: bfloat16 [32, 128, 128], P(('dp', 'vol')), may hold values from -1 to 1
- volume: bfloat16 [256, 256, 256], P('vol'), may hold values from -6 to 6
- line_index: int32 [32, 4, 128], P('dp'), may hold values from 0 to 65278, as said below
- patch_weight: bfloat16 [64, 1024], replicated, may hold values from -0.75 to 0.75
- position: bfloat16 [256, 1024], replicated, may hold values from -3 to 3
- norm_gain: float32 [1024], replicated, may hold values from 0.1 to 1.9
- project_in: bfloat16 [1024, 1536], P('dp'), may hold values from -0.1875 to 0.1875
- project_out: bfloat16 [1024, 512], P('dp'), may hold values from -0.25 to 0.25
- head_weight: float32 [1024, 4], replicated, may hold values from -1.8 to 1.8
Outputs:
- errors: float32 [32, 4], P(('dp', 'vol'))
- in_gradient: float32 [1024, 1536], P('dp')
- out_gradient: float32 [1024, 512], P('dp')
- head_gradient: float32 [1024, 4], replicated
Inputs may be any that keep to these rules, and one draw needn't show every extreme that they name: line_index[i, k, r] = z * 256 + y names the plane z and row y of the volume that row r of hypothesis k of image i samples; z and y lie within 0 and 254.
All inputs are finite; a program needn't handle non-finite values.
Results may differ from a plain program's by a relative error of at most 0.038.
Values may be sent and summed in bfloat16 or wider, within the bound.
A program may use at most 64 MiB of HBM per device.

v0:
```python
import math
import jax
import jax.numpy as jnp
from jax import lax
from jax.sharding import PartitionSpec as P

HEADS = 8
HEAD_DIM = 64
PIX = 128
PATCH = 8
PATCHES = 256
K = 4
EPSILON = 1e-05


def embed_images(images, patch_weight, position):
    count = images.shape[0]
    grid = PIX // PATCH
    pieces = images.reshape(count, grid, PATCH, grid, PATCH).transpose(0, 1, 3, 2, 4)
    pieces = pieces.reshape(count * grid * grid, PATCH * PATCH).astype(jnp.bfloat16)
    mixed = jnp.dot(pieces, patch_weight, preferred_element_type=jnp.float32)
    mixed = mixed.reshape(count, grid * grid, -1) + position.astype(jnp.float32)[None]
    return mixed.reshape(count * grid * grid, -1).astype(jnp.bfloat16)


def normalize(embedded, norm_gain):
    values = embedded.astype(jnp.float32)
    center = values - jnp.mean(values, axis=1, keepdims=True)
    scale = lax.rsqrt(jnp.mean(center * center, axis=1, keepdims=True) + EPSILON)
    return (center * scale * norm_gain[None, :]).astype(jnp.bfloat16)


def attend(triple):
    count = triple.shape[0] // PATCHES
    parts = triple.reshape(count, PATCHES, 3, HEADS, HEAD_DIM).astype(jnp.float32)
    query = parts[:, :, 0]
    keys = parts[:, :, 1]
    values = parts[:, :, 2]
    scores = jnp.einsum("bqhd,bkhd->bhqk", query, keys) * HEAD_DIM ** (-0.5)
    raised = jnp.exp(scores)
    weights = (raised / jnp.sum(raised, axis=-1, keepdims=True)).astype(jnp.bfloat16)
    mixed = jnp.einsum("bhqk,bkhd->bqhd", weights.astype(jnp.float32), values)
    return mixed.reshape(count * PATCHES, HEADS * HEAD_DIM).astype(jnp.bfloat16)


def hartley(images):
    side = images.shape[1]
    freq = jnp.arange(side, dtype=jnp.int32) - side // 2
    place = jnp.arange(side, dtype=jnp.int32)
    phase = (freq[:, None] * place[None, :] % side).astype(jnp.float32) * (2.0 * math.pi / side)
    cosine = jnp.cos(phase)
    sine = jnp.sin(phase)
    highest = lax.Precision.HIGHEST
    first_cos = jnp.einsum("rn,bnm->brm", cosine, images, precision=highest)
    first_sin = jnp.einsum("rn,bnm->brm", sine, images, precision=highest)
    result = jnp.einsum("brm,cm->brc", first_cos, cosine + sine, precision=highest)
    result = result + jnp.einsum("brm,cm->brc", first_sin, cosine - sine, precision=highest)
    return result / side


def render(volume, line_index, slab_index):
    slab, side, _ = volume.shape
    table = volume.reshape(slab * side, side)
    plane = line_index // side - slab_index * slab
    inside = (plane >= 0) & (plane < slab)
    rows = jnp.clip(plane, 0, slab - 1) * side + line_index % side
    picked = jnp.take(table, rows.reshape(-1), axis=0)[:, ::2]
    picked = jnp.where(inside.reshape(-1, 1), picked.astype(jnp.float32), 0.0)
    return (picked.reshape(line_index.shape[0], -1), inside)


def local(
    images,
    contrast,
    volume,
    line_index,
    patch_weight,
    position,
    norm_gain,
    project_in,
    project_out,
    head_weight,
):
    count = images.shape[0]
    width = norm_gain.shape[0]
    highest = lax.Precision.HIGHEST
    rendered, inside = render(volume, line_index, lax.axis_index("vol"))
    spectrum = hartley(images)
    slices = lax.psum_scatter(
        rendered.astype(jnp.bfloat16), "vol", scatter_dimension=0, tiled=True
    ).astype(jnp.float32)
    slices = slices.reshape(count, K, PIX, PIX)
    misfit = contrast.astype(jnp.float32)[:, None] * slices - spectrum[:, None]
    errors = jnp.mean(misfit * misfit, axis=(2, 3))
    embedded = embed_images(images, patch_weight, position)
    normed = normalize(embedded, norm_gain)
    triple = jnp.dot(
        normed,
        lax.all_gather(project_in, "dp", axis=0, tiled=True),
        preferred_element_type=jnp.float32,
    ).astype(jnp.bfloat16)
    attended = attend(triple)
    contract_last = (((1,), (1,)), ((), ()))
    out_whole = lax.all_gather(project_out, "dp", axis=0, tiled=True)
    branch = lax.dot_general(attended, out_whole, contract_last, preferred_element_type=jnp.float32)
    layer_out = embedded.astype(jnp.float32) + branch
    pooled = jnp.mean(layer_out.reshape(count, PATCHES, width), axis=1)
    logits = jnp.dot(pooled, head_weight, precision=highest)
    raised = jnp.exp(logits)
    chances = raised / jnp.sum(raised, axis=1, keepdims=True)
    expected = jnp.sum(chances * errors, axis=1, keepdims=True)
    logit_slope = chances * (errors - expected)
    head_gradient = lax.psum(jnp.dot(pooled.T, logit_slope, precision=highest), ("dp", "vol"))
    pooled_slope = jnp.dot(logit_slope, head_weight.T, precision=highest) / PATCHES
    layer_slope = jnp.broadcast_to(pooled_slope[:, None, :], (count, PATCHES, width))
    layer_slope = layer_slope.reshape(count * PATCHES, width).astype(jnp.bfloat16)
    attended_slope = jnp.dot(layer_slope, out_whole, preferred_element_type=jnp.float32).astype(
        jnp.bfloat16
    )
    triple_slope = jax.vjp(attend, triple)[1](attended_slope)[0]
    contract_first = (((0,), (0,)), ((), ()))
    first = lax.dot_general(
        normed, triple_slope, contract_first, preferred_element_type=jnp.float32
    )
    second = lax.dot_general(
        layer_slope, attended, contract_first, preferred_element_type=jnp.float32
    )
    shard = lax.psum_scatter(
        jnp.concatenate([first, second], axis=1).astype(jnp.bfloat16),
        "dp",
        scatter_dimension=0,
        tiled=True,
    ).astype(jnp.float32)
    shard = lax.psum(shard.astype(jnp.bfloat16), "vol").astype(jnp.float32)
    split = project_in.shape[1]
    return (errors, shard[:, :split], shard[:, split:], head_gradient)


def solution(mesh):
    placed = (
        P(("dp", "vol"), None, None),
        P(("dp", "vol"), None, None),
        P("vol", None, None),
        P("dp", None, None),
        P(),
        P(),
        P(),
        P("dp", None),
        P("dp", None),
        P(),
    )
    return jax.shard_map(
        local,
        mesh=mesh,
        in_specs=placed,
        out_specs=(P(("dp", "vol"), None), P("dp", None), P("dp", None), P()),
        check_vma=False,
    )
```

profile of v0, /device:TPU:0, one launch (start us, length us, event | category | flops | bytes accessed | tf_op | source)
XLA Modules:
  0.0 261.4 jit_solution(18446166115794627641)
XLA Ops:
  8.0 0.0 copy-start
  8.0 0.0 all-reduce.9.cloned.1.call-start
  8.1 0.7 fusion.38
  8.8 0.7 compare_and_fusion.1
  9.5 11.4 %gather_fusion = bf16[1024,256]{1,0:T(8,128)(2,1)S(1)} fusion(bf16[32768,256]{1,0:T(8,128)(2,1)} %bitcast.106, s32[1024]{0:T(1024)S(1)} %broadcast_clamp_fusion), kind=kCustom, calls=%fused_computation | custom fusion | bytes 1052672 | tf_op jit(solution)/shard_map/jit(_take)/gather | solution.py:67
  21.0 0.2 broadcast_select_fusion
  21.2 10.3 %slice.21 = bf16[1024,128]{1,0:T(8,128)(2,1)S(1)} slice(bf16[1024,256]{1,0:T(8,128)(2,1)S(1)} %broadcast_select_fusion), slice={[0:1024:1], [0:256:2]} | slice | bytes 524288 | tf_op jit(solution)/shard_map/slice | solution.py:67
  31.5 0.2 select_convert_fusion
  31.7 0.8 convert_element_type.102
  32.5 0.0 all-reduce.9.cloned.1.call-update
  32.5 0.0 all-gather.3.cloned.1.call-start
  32.5 0.5 all-gather.3.cloned.1.call-update
  33.1 0.0 all-gather.5.cloned.1.call-start
  33.1 0.5 all-gather.5.cloned.1.call-update
  33.6 0.2 reduce-scatter.2.cloned.1.call-start
  33.9 0.5 fusion.21
  34.4 0.0 copy-start.22
  34.4 0.5 fusion.19
  35.0 0.6 fusion.24
  35.6 0.6 convert_element_type.105
  36.2 0.3 copy.31
  36.5 0.2 convert_element_type.107
  36.7 0.4 convert_reduce_fusion
  37.2 0.3 fusion.11
  37.5 0.6 dynamic-slice
  38.1 0.6 fusion.9
  38.7 19.9 %all-reduce.9.cloned.1.call-done = bf16[2,65536]{1,0:T(2,128)(2,1)} async-done(((bf16[2,65536]{1,0:T(2,128)(2,1)}), bf16[2,65536]{1,0:T(2,128)(2,1)}) %all-reduce.9.cloned.1.call-update) | async-done | bytes 262160
  58.6 1.8 dynamic-slice_convert_fusion
  60.4 0.6 multiply_reduce_fusion
  61.0 22.6 %all-gather.3.cloned.1.call-done = bf16[1024,1536]{1,0:T(8,128)(2,1)} async-done(((bf16[64,1536]{1,0:T(8,128)(2,1)}), bf16[1024,1536]{1,0:T(8,128)(2,1)}) %all-gather.3.cloned.1.call-update) | async-done | bytes 3145744 | tf_op jit(solution)/shard_map/all_gather | solution.py:99
  83.7 3.0 %convolution_convert_fusion.1 = bf16[256,1536]{1,0:T(8,128)(2,1)S(1)} fusion(bf16[1024,1536]{1,0:T(8,128)(2,1)} %all-gather.3.cloned.1.call-done, bf16[256,1024]{1,0:T(8,128)(2,1)S(1)} %get-tuple-element.9, f32[1024]{0:T(1024)S(1)} %copy-done.17, f32[256]{0:T(256)S(1)} %add_rsqrt_fusion, f32[256]{0:T(256)S(1)} %broadcast_multiply_fusion.2), kind=kOutput, calls=%fused_computation.5 | convolution fusion | flops 807010304 | bytes 4462592 | tf_op jit(solution)/shard_map/dot_general | solution.py:97
  86.7 0.3 copy.32
  87.0 0.5 fusion.63
  87.5 0.3 copy-done.3
  87.9 0.2 divide_convert_fusion
  88.0 1.2 convolution_convert_fusion.5
  89.3 32.9 %all-gather.5.cloned.1.call-done = bf16[1024,512]{1,0:T(8,128)(2,1)} async-done(((bf16[64,512]{1,0:T(8,128)(2,1)}), bf16[1024,512]{1,0:T(8,128)(2,1)}) %all-gather.5.cloned.1.call-update) | async-done | bytes 1048592 | tf_op jit(solution)/shard_map/all_gather | solution.py:104
  122.2 1.9 fusion.8
  124.2 0.8 fusion.64
  125.0 1.3 multiply_reduce_fusion.1
  126.3 1.2 subtract_multiply_fusion
  127.5 0.2 fusion.40
  127.7 0.0 copy-done.10
  127.7 0.4 copy-done.15
  128.1 1.5 convolution_convert_fusion.3
  129.6 1.1 convolution_convert_fusion.4
  130.7 1.1 copy.34
  131.8 1.5 fusion.4
  133.4 0.6 convolution_bitcast_fusion
  134.0 0.6 convolution_bitcast_fusion.1
  134.6 0.4 convolution_bitcast_fusion.2
  135.0 0.1 add_convert_fusion
  135.1 0.5 copy-done.2
  135.6 1.2 convolution_convert_fusion
  136.8 0.0 copy-done.5
  136.8 2.6 pad_maximum_fusion
  139.4 0.0 reduce-scatter.2.cloned.1.call-update
  139.4 0.0 all-reduce.7.cloned.1.call-start
  139.5 71.4 %reduce-scatter.2.cloned.1.call-done = bf16[64,2048]{1,0:T(8,128)(2,1)} async-done(((bf16[1024,2048]{1,0:T(8,128)(2,1)}), bf16[64,2048]{1,0:T(8,128)(2,1)}) %reduce-scatter.2.cloned.1.call-update) | async-done | bytes 262160 | tf_op jit(solution)/shard_map/reduce_scatter | solution.py:128
  210.9 0.0 all-reduce.7.cloned.1.call-update
  210.9 0.1 broadcast_multiply_fusion
  211.0 39.6 %psum.15 = f32[1024,4]{0,1:T(4,128)} all-reduce(f32[1024,4]{0,1:T(4,128)S(1)} %broadcast_multiply_fusion), channel_id=1, replica_groups=mesh['dp'=16,'vol'=2] {'dp','vol'}, use_global_device_ids=true, to_apply=%region_11.12 | all-reduce | flops 4096 | bytes 32768 | tf_op jit(solution)/shard_map/psum | solution.py:113
  250.6 1.7 slice.32
  252.3 1.5 slice.33
  (52 shorter events, 0.2 us)
Async XLA Ops:
  8.0 28.7 %copy-start = (bf16[64,1024]{1,0:T(8,128)(2,1)S(1)}, bf16[64,1024]{1,0:T(8,128)(2,1)}, u32[]{:S(2)}) copy-start(bf16[64,1024]{1,0:T(8,128)(2,1)} %param.14) | copy-start | bytes 393220
  8.0 50.5 %all-reduce.9.cloned.1.call-start = ((), (), s32[]{:S(2)}) async-start(), calls=%async_computation.5 | async-start | bytes 524288
  20.9 13.0 %copy-start.7 = (f32[1,128,128]{2,1,0:T(8,128)S(1)}, f32[1,128,128]{2,1,0:T(8,128)}, u32[]{:S(2)}) copy-start(f32[1,128,128]{2,1,0:T(8,128)} %param.10) | copy-start | bytes 196612
  21.0 14.6 %copy-start.8 = (bf16[1,128,128]{2,1,0:T(8,128)(2,1)S(1)}, bf16[1,128,128]{2,1,0:T(8,128)(2,1)}, u32[]{:S(2)}) copy-start(bf16[1,128,128]{2,1,0:T(8,128)(2,1)} %param.11) | copy-start | bytes 98308
  31.5 5.3 %copy-start.6 = (bf16[256,1024]{1,0:T(8,128)(2,1)S(1)}, bf16[256,1024]{1,0:T(8,128)(2,1)}, u32[]{:S(2)}) copy-start(bf16[256,1024]{1,0:T(8,128)(2,1)} %param.15) | copy-start | bytes 1572868
  32.5 51.2 %all-gather.3.cloned.1.call-start = ((), (), s32[]{:S(2)}) async-start(), calls=%async_computation.1 | async-start | bytes 3342336 | tf_op jit(solution)/shard_map/all_gather | solution.py:99
  33.1 89.2 %all-gather.5.cloned.1.call-start = ((), (), s32[]{:S(2)}) async-start(), calls=%async_computation.2 | async-start | bytes 1114112 | tf_op jit(solution)/shard_map/all_gather | solution.py:104
  33.6 177.2 %reduce-scatter.2.cloned.1.call-start = ((), (), s32[]{:S(2)}) async-start(), calls=%async_computation.3 | async-start | bytes 4456448 | tf_op jit(solution)/shard_map/reduce_scatter | solution.py:128
  34.4 3.1 %copy-start.22 = (u32[32]{0:T(128)S(1)}, u32[32]{0:T(128)}, u32[]{:S(2)}) copy-start(u32[32]{0:T(128)} %constant.104) | copy-start | bytes 388
  36.2 47.5 %copy-start.17 = (f32[1024]{0:T(1024)S(1)}, f32[1024]{0:T(1024)}, u32[]{:S(2)}) copy-start(f32[1024]{0:T(1024)} %param.16) | copy-start | bytes 12292
  37.2 49.5 %copy-start.1 = (bf16[256,1024]{1,0:T(8,128)(2,1)}, bf16[256,1024]{1,0:T(8,128)(2,1)S(1)}, u32[]{:S(2)}) copy-start(bf16[256,1024]{1,0:T(8,128)(2,1)S(1)} %get-tuple-element.9) | copy-start | bytes 1572868
  37.2 49.5 %copy-start.12 = (f32[256]{0:T(256)}, f32[256]{0:T(256)S(1)}, u32[]{:S(2)}) copy-start(f32[256]{0:T(256)S(1)} %broadcast_multiply_fusion.2) | copy-start | bytes 3076
  37.5 49.2 %copy-start.19 = (f32[256]{0:T(256)}, f32[256]{0:T(256)S(1)}, u32[]{:S(2)}) copy-start(f32[256]{0:T(256)S(1)} %add_rsqrt_fusion) | copy-start | bytes 3076
  87.0 0.9 copy-start.3
  122.2 2.0 copy-start.9
  122.2 2.8 %copy-start.14 = (f32[4]{0:T(128)S(1)}, f32[4]{0:T(128)}, u32[]{:S(2)}) copy-start(f32[4]{0:T(128)} %multiply_reduce_fusion) | copy-start | bytes 52
  122.2 7.4 %copy-start.21 = (bf16[1024,512]{1,0:T(8,128)(2,1)S(1)}, bf16[1024,512]{1,0:T(8,128)(2,1)}, u32[]{:S(2)}) copy-start(bf16[1024,512]{1,0:T(8,128)(2,1)} %all-gather.5.cloned.1.call-done) | copy-start | bytes 3145732
  124.2 3.5 %copy-start.10 = (f32[1024]{0:T(1024)}, f32[1024]{0:T(1024)S(1)}, u32[]{:S(2)}) copy-start(f32[1024]{0:T(1024)S(1)} %broadcast_multiply_fusion.1) | copy-start | bytes 12292
  127.5 0.6 copy-start.15
  131.8 1.6 copy-start.4
  134.6 1.0 copy-start.2
  134.6 1.0 copy-start.13
  134.6 1.0 copy-start.18
  134.6 1.0 copy-start.20
  135.6 1.2 copy-start.5
  139.4 71.5 %copy-start.11 = (f32[1024]{0:T(1024)S(1)}, f32[1024]{0:T(1024)}, u32[]{:S(2)}) copy-start(f32[1024]{0:T(1024)} %copy-done.10) | copy-start | bytes 12292
  139.4 71.5 %copy-start.16 = (f32[4]{0:T(128)S(1)}, f32[4]{0:T(128)}, u32[]{:S(2)}) copy-start(f32[4]{0:T(128)} %copy-done.15) | copy-start | bytes 52
  139.4 111.2 %all-reduce.7.cloned.1.call-start = ((), (), s32[]{:S(2)}) async-start(), calls=%async_computation.4 | async-start | bytes 524288 | tf_op jit(solution)/shard_map/psum | solution.py:134
Sparse Core Ops, SparseCore 0:
  32.6 25.9 all-reduce.8
  211.0 22.3 all-reduce.6
Sparse Core Ops, SparseCore 1:
  35.5 48.1 all-gather.2
  85.9 36.2 all-gather.4
  139.5 71.3 reduce-scatter.1
where the time goes:
time: 262 us; the launch traced here: 261 us
  waiting for transfers between devices  148 us (56%)
  blocking collectives  39.6 us (15%)
  local copies, waits for them, and re-layouts  30.1 us (11%)
  matrix products  17.1 us (7%)
  between operations  16.1 us (6%)
  other arithmetic  10.1 us (4%)
    reduce_scatter x1, waiting for transfers between devices, local(): lax.psum_scatter(jnp.concatenate([first, second], axis=1).astype(jnp.bflo...  71.4 us
    psum x1, blocking collectives, local(): lax.psum(jnp.dot(pooled.T, logit_slope, precision=highest), ('dp', 'vol'))  39.6 us
    all_gather x1, waiting for transfers between devices, local(): out_whole = lax.all_gather(project_out, 'dp', axis=0, tiled=True)  32.9 us
    all_gather x1, waiting for transfers between devices, local(): lax.all_gather(project_in, 'dp', axis=0, tiled=True)  22.6 us
    unnamed x6, waiting for transfers between devices  21 us
    gather x1, local copies, waits for them, and re-layouts, render(): picked = jnp.take(table, rows.reshape(-1), axis=0)[:, ::2]  11.4 us
    slice x1, local copies, waits for them, and re-layouts, render(): picked = jnp.take(table, rows.reshape(-1), axis=0)[:, ::2]  10.3 us
  transfers between devices with their start and end apart: 5, of which 4 were waited for; matrix products, arithmetic and copies ran while one was open for 5% of the time, Pallas kernels for 0%

commit v1 on v0

--- a/solution.py
+++ b/solution.py
@@ -110,7 +110,8 @@
     chances = raised / jnp.sum(raised, axis=1, keepdims=True)
     expected = jnp.sum(chances * errors, axis=1, keepdims=True)
     logit_slope = chances * (errors - expected)
-    head_gradient = lax.psum(jnp.dot(pooled.T, logit_slope, precision=highest), ("dp", "vol"))
+    one_axis = lax.psum(jnp.dot(pooled.T, logit_slope, precision=highest), "vol")
+    head_gradient = lax.psum(one_axis, "dp")
     pooled_slope = jnp.dot(logit_slope, head_weight.T, precision=highest) / PATCHES
     layer_slope = jnp.broadcast_to(pooled_slope[:, None, :], (count, PATCHES, width))
     layer_slope = layer_slope.reshape(count * PATCHES, width).astype(jnp.bfloat16)

time: 262 us -> 288 us (1.099)
  blocking collectives: 39.6 us -> 65.6 us
    psum x1 -> x2, blocking collectives: 39.6 us -> 65.6 us  [the longest x1 57.6 us: local(): head_gradient = lax.psum(one_axis, 'dp')]
  transfers between devices with their start and end apart: 5 -> 5, of which waited for: 4 -> 4; matrix products, arithmetic and copies ran while one was open for 5% -> 4% of each run, Pallas kernels for 0% -> 0%
where the time goes in v1:
time: 288 us; the launch traced here: 287 us
  waiting for transfers between devices  148 us (51%)
  blocking collectives  65.6 us (23%)
  local copies, waits for them, and re-layouts  30 us (10%)
  matrix products  17.1 us (6%)
  between operations  16.1 us (6%)
  other arithmetic  10 us (3%)
    reduce_scatter x1, waiting for transfers between devices, local(): lax.psum_scatter(jnp.concatenate([first, second], axis=1).astype(jnp.bflo...  71.4 us
    psum x1, blocking collectives, local(): head_gradient = lax.psum(one_axis, 'dp')  57.6 us
    all_gather x1, waiting for transfers between devices, local(): out_whole = lax.all_gather(project_out, 'dp', axis=0, tiled=True)  32.9 us
    all_gather x1, waiting for transfers between devices, local(): lax.all_gather(project_in, 'dp', axis=0, tiled=True)  22.6 us
    unnamed x6, waiting for transfers between devices  21 us
    gather x1, local copies, waits for them, and re-layouts, render(): picked = jnp.take(table, rows.reshape(-1), axis=0)[:, ::2]  11.4 us
    slice x1, local copies, waits for them, and re-layouts, render(): picked = jnp.take(table, rows.reshape(-1), axis=0)[:, ::2]  10.3 us
    psum x1, blocking collectives, local(): lax.psum(jnp.dot(pooled.T, logit_slope, precision=highest), 'vol')  8.01 us
  transfers between devices with their start and end apart: 5, of which 4 were waited for; matrix products, arithmetic and copies ran while one was open for 4% of the time, Pallas kernels for 0%

profile of v1, /device:TPU:0, one launch (start us, length us, event | category | flops | bytes accessed | tf_op | source)
XLA Modules:
  0.0 287.3 jit_solution(14178335303161701951)
XLA Ops:
  8.0 0.0 copy-start
  8.0 0.0 all-reduce.9.cloned.1.call-start
  8.1 0.7 fusion.38
  8.8 0.7 compare_and_fusion.1
  9.5 11.4 %gather_fusion = bf16[1024,256]{1,0:T(8,128)(2,1)S(1)} fusion(bf16[32768,256]{1,0:T(8,128)(2,1)} %bitcast.106, s32[1024]{0:T(1024)S(1)} %broadcast_clamp_fusion), kind=kCustom, calls=%fused_computation | custom fusion | bytes 1052672 | tf_op jit(solution)/shard_map/jit(_take)/gather | solution.py:67
  21.0 0.2 broadcast_select_fusion
  21.2 10.3 %slice.21 = bf16[1024,128]{1,0:T(8,128)(2,1)S(1)} slice(bf16[1024,256]{1,0:T(8,128)(2,1)S(1)} %broadcast_select_fusion), slice={[0:1024:1], [0:256:2]} | slice | bytes 524288 | tf_op jit(solution)/shard_map/slice | solution.py:67
  31.5 0.2 select_convert_fusion
  31.7 0.8 convert_element_type.102
  32.5 0.0 all-reduce.9.cloned.1.call-update
  32.5 0.0 all-gather.3.cloned.1.call-start
  32.5 0.5 all-gather.3.cloned.1.call-update
  33.1 0.0 all-gather.5.cloned.1.call-start
  33.1 0.5 all-gather.5.cloned.1.call-update
  33.6 0.2 reduce-scatter.2.cloned.1.call-start
  33.9 0.5 fusion.21
  34.4 0.5 fusion.19
  35.0 0.6 fusion.24
  35.6 0.6 convert_element_type.105
  36.2 0.3 copy.31
  36.5 0.2 convert_element_type.107
  36.7 0.4 convert_reduce_fusion
  37.2 0.3 fusion.11
  37.5 0.6 dynamic-slice
  38.1 0.6 fusion.9
  38.7 19.9 %all-reduce.9.cloned.1.call-done = bf16[2,65536]{1,0:T(2,128)(2,1)} async-done(((bf16[2,65536]{1,0:T(2,128)(2,1)}), bf16[2,65536]{1,0:T(2,128)(2,1)}) %all-reduce.9.cloned.1.call-update) | async-done | bytes 262160
  58.6 1.8 dynamic-slice_convert_fusion
  60.4 0.6 multiply_reduce_fusion
  61.0 22.6 %all-gather.3.cloned.1.call-done = bf16[1024,1536]{1,0:T(8,128)(2,1)} async-done(((bf16[64,1536]{1,0:T(8,128)(2,1)}), bf16[1024,1536]{1,0:T(8,128)(2,1)}) %all-gather.3.cloned.1.call-update) | async-done | bytes 3145744 | tf_op jit(solution)/shard_map/all_gather | solution.py:99
  83.7 3.0 %convolution_convert_fusion.1 = bf16[256,1536]{1,0:T(8,128)(2,1)S(1)} fusion(bf16[1024,1536]{1,0:T(8,128)(2,1)} %all-gather.3.cloned.1.call-done, bf16[256,1024]{1,0:T(8,128)(2,1)S(1)} %get-tuple-element.9, f32[1024]{0:T(1024)S(1)} %copy-done.17, f32[256]{0:T(256)S(1)} %add_rsqrt_fusion, f32[256]{0:T(256)S(1)} %broadcast_multiply_fusion.2), kind=kOutput, calls=%fused_computation.5 | convolution fusion | flops 807010304 | bytes 4462592 | tf_op jit(solution)/shard_map/dot_general | solution.py:97
  86.7 0.3 copy.32
  87.0 0.5 fusion.63
  87.5 0.3 copy-done.3
  87.9 0.2 divide_convert_fusion
  88.0 1.2 convolution_convert_fusion.5
  89.3 32.9 %all-gather.5.cloned.1.call-done = bf16[1024,512]{1,0:T(8,128)(2,1)} async-done(((bf16[64,512]{1,0:T(8,128)(2,1)}), bf16[1024,512]{1,0:T(8,128)(2,1)}) %all-gather.5.cloned.1.call-update) | async-done | bytes 1048592 | tf_op jit(solution)/shard_map/all_gather | solution.py:104
  122.2 1.9 fusion.8
  124.2 0.8 fusion.64
  125.0 1.3 multiply_reduce_fusion.1
  126.3 1.1 subtract_multiply_fusion
  127.4 0.2 fusion.40
  127.6 0.0 copy-done.10
  127.6 0.4 copy-done.15
  128.0 1.5 convolution_convert_fusion.3
  129.4 1.1 convolution_convert_fusion.4
  130.6 1.1 copy.34
  131.7 1.5 fusion.4
  133.2 0.6 convolution_bitcast_fusion
  133.8 0.6 convolution_bitcast_fusion.1
  134.4 0.4 convolution_bitcast_fusion.2
  134.9 0.1 add_convert_fusion
  135.0 0.5 copy-done.2
  135.5 1.2 convolution_convert_fusion
  136.7 0.0 copy-done.5
  136.7 2.6 pad_maximum_fusion
  139.3 0.0 reduce-scatter.2.cloned.1.call-update
  139.3 0.0 all-reduce.7.cloned.1.call-start
  139.3 71.4 %reduce-scatter.2.cloned.1.call-done = bf16[64,2048]{1,0:T(8,128)(2,1)} async-done(((bf16[1024,2048]{1,0:T(8,128)(2,1)}), bf16[64,2048]{1,0:T(8,128)(2,1)}) %reduce-scatter.2.cloned.1.call-update) | async-done | bytes 262160 | tf_op jit(solution)/shard_map/reduce_scatter | solution.py:129
  210.8 0.0 all-reduce.7.cloned.1.call-update
  210.8 0.1 broadcast_multiply_fusion
  210.9 8.0 %psum.22 = f32[1024,4]{0,1:T(4,128)S(1)} all-reduce(f32[1024,4]{0,1:T(4,128)S(1)} %broadcast_multiply_fusion), channel_id=1, replica_groups=mesh['dp'=16,'vol'=2] {'vol'}, use_global_device_ids=true, to_apply=%region_11.12 | all-reduce | flops 4096 | bytes 32768 | tf_op jit(solution)/shard_map/psum | solution.py:113
  218.9 57.6 %psum.23 = f32[1024,4]{0,1:T(4,128)} all-reduce(f32[1024,4]{0,1:T(4,128)S(1)} %psum.22), channel_id=1, replica_groups=mesh['dp'=16,'vol'=2] {'dp'}, use_global_device_ids=true, to_apply=%region_12.13 | all-reduce | flops 4096 | bytes 32768 | tf_op jit(solution)/shard_map/psum | solution.py:114
  276.5 1.7 slice.32
  278.2 1.5 slice.33
  (53 shorter events, 0.2 us)
Async XLA Ops:
  8.0 28.7 %copy-start = (bf16[64,1024]{1,0:T(8,128)(2,1)S(1)}, bf16[64,1024]{1,0:T(8,128)(2,1)}, u32[]{:S(2)}) copy-start(bf16[64,1024]{1,0:T(8,128)(2,1)} %param.14) | copy-start | bytes 393220
  8.0 50.5 %all-reduce.9.cloned.1.call-start = ((), (), s32[]{:S(2)}) async-start(), calls=%async_computation.5 | async-start | bytes 524288
  20.9 13.0 %copy-start.7 = (f32[1,128,128]{2,1,0:T(8,128)S(1)}, f32[1,128,128]{2,1,0:T(8,128)}, u32[]{:S(2)}) copy-start(f32[1,128,128]{2,1,0:T(8,128)} %param.10) | copy-start | bytes 196612
  21.0 14.6 %copy-start.8 = (bf16[1,128,128]{2,1,0:T(8,128)(2,1)S(1)}, bf16[1,128,128]{2,1,0:T(8,128)(2,1)}, u32[]{:S(2)}) copy-start(bf16[1,128,128]{2,1,0:T(8,128)(2,1)} %param.11) | copy-start | bytes 98308
  31.5 5.3 %copy-start.6 = (bf16[256,1024]{1,0:T(8,128)(2,1)S(1)}, bf16[256,1024]{1,0:T(8,128)(2,1)}, u32[]{:S(2)}) copy-start(bf16[256,1024]{1,0:T(8,128)(2,1)} %param.15) | copy-start | bytes 1572868
  32.5 51.2 %all-gather.3.cloned.1.call-start = ((), (), s32[]{:S(2)}) async-start(), calls=%async_computation.1 | async-start | bytes 3342336 | tf_op jit(solution)/shard_map/all_gather | solution.py:99
  33.1 89.2 %all-gather.5.cloned.1.call-start = ((), (), s32[]{:S(2)}) async-start(), calls=%async_computation.2 | async-start | bytes 1114112 | tf_op jit(solution)/shard_map/all_gather | solution.py:104
  33.6 177.1 %reduce-scatter.2.cloned.1.call-start = ((), (), s32[]{:S(2)}) async-start(), calls=%async_computation.3 | async-start | bytes 4456448 | tf_op jit(solution)/shard_map/reduce_scatter | solution.py:129
  34.4 3.1 %copy-start.22 = (u32[32]{0:T(128)S(1)}, u32[32]{0:T(128)}, u32[]{:S(2)}) copy-start(u32[32]{0:T(128)} %constant.104) | copy-start | bytes 388
  36.2 47.5 %copy-start.17 = (f32[1024]{0:T(1024)S(1)}, f32[1024]{0:T(1024)}, u32[]{:S(2)}) copy-start(f32[1024]{0:T(1024)} %param.16) | copy-start | bytes 12292
  37.2 49.5 %copy-start.1 = (bf16[256,1024]{1,0:T(8,128)(2,1)}, bf16[256,1024]{1,0:T(8,128)(2,1)S(1)}, u32[]{:S(2)}) copy-start(bf16[256,1024]{1,0:T(8,128)(2,1)S(1)} %get-tuple-element.9) | copy-start | bytes 1572868
  37.2 49.5 %copy-start.12 = (f32[256]{0:T(256)}, f32[256]{0:T(256)S(1)}, u32[]{:S(2)}) copy-start(f32[256]{0:T(256)S(1)} %broadcast_multiply_fusion.2) | copy-start | bytes 3076
  37.5 49.2 %copy-start.19 = (f32[256]{0:T(256)}, f32[256]{0:T(256)S(1)}, u32[]{:S(2)}) copy-start(f32[256]{0:T(256)S(1)} %add_rsqrt_fusion) | copy-start | bytes 3076
  87.0 0.9 copy-start.3
  122.2 2.0 copy-start.9
  122.2 2.8 copy-start.14
  122.2 7.2 %copy-start.21 = (bf16[1024,512]{1,0:T(8,128)(2,1)S(1)}, bf16[1024,512]{1,0:T(8,128)(2,1)}, u32[]{:S(2)}) copy-start(bf16[1024,512]{1,0:T(8,128)(2,1)} %all-gather.5.cloned.1.call-done) | copy-start | bytes 3145732
  124.2 3.4 %copy-start.10 = (f32[1024]{0:T(1024)}, f32[1024]{0:T(1024)S(1)}, u32[]{:S(2)}) copy-start(f32[1024]{0:T(1024)S(1)} %broadcast_multiply_fusion.1) | copy-start | bytes 12292
  127.4 0.5 copy-start.15
  131.7 1.6 copy-start.4
  134.4 1.0 copy-start.2
  134.4 1.0 copy-start.13
  134.4 1.0 copy-start.18
  134.4 1.0 copy-start.20
  135.5 1.2 copy-start.5
  139.3 71.5 %copy-start.11 = (f32[1024]{0:T(1024)S(1)}, f32[1024]{0:T(1024)}, u32[]{:S(2)}) copy-start(f32[1024]{0:T(1024)} %copy-done.10) | copy-start | bytes 12292
  139.3 71.6 %copy-start.16 = (f32[4]{0:T(128)S(1)}, f32[4]{0:T(128)}, u32[]{:S(2)}) copy-start(f32[4]{0:T(128)} %copy-done.15) | copy-start | bytes 52
  139.3 137.2 %all-reduce.7.cloned.1.call-start = ((), (), s32[]{:S(2)}) async-start(), calls=%async_computation.4 | async-start | bytes 524288 | tf_op jit(solution)/shard_map/psum | solution.py:135
Sparse Core Ops, SparseCore 0:
  32.6 25.9 all-reduce.8
  210.9 22.2 all-reduce.6
Sparse Core Ops, SparseCore 1:
  35.5 48.1 all-gather.2
  85.9 36.2 all-gather.4
  139.4 71.4 reduce-scatter.1
